TPU v7x, 128 devices: a whole 4x4x4 slice. The times are simulated.
128 devices in a mesh: dp: 8 (over z, core), table: 16 (over x, y).
Axes of the slice: x: 4, y: 4, z: 4, core: 2. Of those that a mesh axis runs over, the one named last changes fastest.
Arguments:
- values: bfloat16 [16384, 1024], P('table'), may hold values from -6 to 6
- first_moment: float32 [16384, 1024], P('table'), may hold values from -2 to 2
- second_moment: float32 [16384, 1024], P('table'), may hold values from 0.01 to 1
- grads: bfloat16 [1024, 64, 1024], P(('dp', 'table')), may hold values from -6 to 6
- block_ids: int32 [128, 8], P(('dp', 'table')), may hold values from 0 to 255, as said below
- live_counts: int32 [128], P(('dp', 'table')), may hold values from 4 to 8
- step_count: int32 [1], replicated, may hold values from 1 to 19
Outputs:
- new_values: bfloat16 [16384, 1024], P('table')
- new_first: float32 [16384, 1024], P('table')
- new_second: float32 [16384, 1024], P('table')
Inputs may be any that keep to these rules, and one draw needn't show every extreme that they name: `block_ids`: device h belongs to replica h // 16. Live ids of a device are ascending and lie in blocks of different owners (owner = id // 16), so one device sends at most one live block to any owner; in every draw some owner receives a live block from every device of a replica. The live ids of one replica name at most 2 different blocks of any one owner, and exactly 2 of some owner in every replica. Ids of dead slots are arbitrary blocks.
All inputs are finite; a program needn't handle non-finite values.
Results may differ from a plain program's by a relative error of at most 0.0004.
Values may be sent and summed in bfloat16 or wider, within the bound.
A program may use at most 128 MiB of HBM per device.

v0:
```python
import jax
import jax.numpy as jnp
from jax import lax
from jax.sharding import PartitionSpec as P

BROWS = 64
SLOTS = 8
KBLK = 2


def adam_rows(values, first_moment, second_moment, row_grad, row_hits, step_count):
    touched = (row_hits > 0.0)[:, None]
    beta_one = 0.9
    beta_two = 0.99
    steps_done = step_count[0].astype(jnp.float32)
    first_next = beta_one * first_moment + (1.0 - beta_one) * row_grad
    second_next = beta_two * second_moment + (1.0 - beta_two) * row_grad * row_grad
    first_hat = first_next / (1.0 - jnp.power(jnp.float32(beta_one), steps_done))
    second_hat = second_next / (1.0 - jnp.power(jnp.float32(beta_two), steps_done))
    moved = values.astype(jnp.float32) - 0.05 * first_hat / (jnp.sqrt(second_hat) + 1e-08)
    new_values = jnp.where(touched, moved.astype(jnp.bfloat16), values)
    new_first = jnp.where(touched, first_next, first_moment)
    new_second = jnp.where(touched, second_next, second_moment)
    return (new_values, new_first, new_second)


def per_device(values, first_moment, second_moment, grads, block_ids, live_counts, step_count):
    owners = lax.axis_size("table")
    own_rows = values.shape[0]
    width = values.shape[1]
    blk_here = own_rows // BROWS
    slot_ids = block_ids[0]
    live = jnp.arange(SLOTS, dtype=jnp.int32) < live_counts[0]
    owner_of = slot_ids // blk_here
    local_block = slot_ids % blk_here
    select = (owner_of[None, :] == jnp.arange(owners, dtype=jnp.int32)[:, None]) & live[None, :]
    outgoing = jnp.einsum(
        "os,sxd->oxd", select.astype(jnp.bfloat16), grads, preferred_element_type=jnp.float32
    ).astype(jnp.bfloat16)
    select_int = select.astype(jnp.int32)
    labels = jnp.stack(
        [jnp.sum(select_int * local_block[None, :], axis=1), jnp.sum(select_int, axis=1)], axis=1
    )
    incoming, arrived = (
        lax.all_to_all(outgoing, "table", split_axis=0, concat_axis=0, tiled=True),
        lax.all_to_all(labels, "table", split_axis=0, concat_axis=0, tiled=True),
    )
    matches = (arrived[:, 0][None, :] == jnp.arange(blk_here, dtype=jnp.int32)[:, None]) & (
        arrived[:, 1][None, :] == 1
    )
    block_hits = jnp.sum(matches.astype(jnp.float32), axis=1)
    touched_block = block_hits > 0.0
    order = jnp.cumsum(touched_block.astype(jnp.int32)) - 1
    packing = (
        (order[None, :] == jnp.arange(KBLK, dtype=jnp.int32)[:, None]) & touched_block[None, :]
    ).astype(jnp.float32)
    chooser = jnp.dot(packing, matches.astype(jnp.float32), precision=lax.Precision.HIGHEST).astype(
        jnp.bfloat16
    )
    packed = jnp.einsum("ks,sxd->kxd", chooser, incoming, preferred_element_type=jnp.float32)
    block_index = jnp.arange(blk_here, dtype=jnp.float32)
    packed_ids = jnp.sum(packing * (block_index[None, :] + 1.0), axis=1) - 1.0
    packed_hits = jnp.sum(packing * block_hits[None, :], axis=1)
    all_packed, all_ids, all_hits = (
        lax.all_gather(packed, "dp", axis=0, tiled=True),
        lax.all_gather(packed_ids, "dp", axis=0, tiled=True),
        lax.all_gather(packed_hits, "dp", axis=0, tiled=True),
    )
    placing = (all_ids[None, :] == block_index[:, None]).astype(jnp.float32)
    row_grad = jnp.einsum(
        "bk,kxd->bxd", placing, all_packed, precision=lax.Precision.HIGHEST
    ).reshape(own_rows, width)
    total_hits = jnp.repeat(jnp.sum(placing * all_hits[None, :], axis=1), BROWS)
    return adam_rows(values, first_moment, second_moment, row_grad, total_hits, step_count)


def solution(mesh):
    in_specs = (
        P("table", None),
        P("table", None),
        P("table", None),
        P(("dp", "table"), None, None),
        P(("dp", "table"), None),
        P(("dp", "table")),
        P(),
    )
    out_specs = (P("table", None), P("table", None), P("table", None))
    return jax.shard_map(
        per_device, mesh=mesh, in_specs=in_specs, out_specs=out_specs, check_vma=False
    )
```

profile of v0, /device:TPU:1, one launch (start us, length us, event | category | flops | bytes accessed | tf_op | source)
XLA Modules:
  0.0 118.3 jit_solution(3008917598142463513)
XLA Ops:
  7.2 0.0 copy-start
  7.9 0.7 fusion.24
  8.6 0.1 select_reduce_fusion.1
  8.7 0.7 copy.29
  9.4 7.6 %all-to-all-start = ((s32[16,1,2]{2,1,0:T(1,128)}), s32[16,1,2]{2,1,0:T(1,128)S(1)}, u32[]{:S(2)}, u32[]{:S(2)}) async-start(s32[16,1,2]{2,1,0:T(1,128)} %copy.29), calls=%async_computation | async-start | bytes 16384 | tf_op jit(solution)/shard_map/all_to_all | solution.py:46
  17.0 0.0 copy-done
  17.0 0.9 convolution_convert_fusion
  17.9 2.5 %copy.33 = bf16[16,64,1024]{2,1,0:T(8,128)(2,1)} copy(bf16[16,64,1024]{2,0,1:T(8,128)(2,1)S(1)} %convolution_convert_fusion) | data formatting | bytes 4194304 | tf_op jit(solution)/shard_map/convert_element_type | solution.py:39
  20.4 0.0 copy-start.4
  20.4 2.9 %all-to-all-done = s32[16,1,2]{2,1,0:T(1,128)S(1)} async-done(((s32[16,1,2]{2,1,0:T(1,128)}), s32[16,1,2]{2,1,0:T(1,128)S(1)}, u32[]{:S(2)}, u32[]{:S(2)}) %all-to-all-start) | async-done | bytes 160 | tf_op jit(solution)/shard_map/all_to_all | solution.py:46
  23.3 3.9 %all-to-all-start.1 = ((bf16[16,64,1024]{2,1,0:T(8,128)(2,1)}), bf16[16,64,1024]{2,1,0:T(8,128)(2,1)S(1)}, u32[]{:S(2)}, u32[]{:S(2)}) async-start(bf16[16,64,1024]{2,1,0:T(8,128)(2,1)} %copy.33), calls=%async_computation.1 | async-start | bytes 4194304 | tf_op jit(solution)/shard_map/all_to_all | solution.py:45
  27.2 0.0 all-gather.2.cloned.1.call-start
  27.2 0.1 copy.30
  27.3 0.1 convert_reduce_fusion
  27.4 0.1 copy.31
  27.6 0.1 add_reduce_fusion
  27.7 0.1 fusion.9
  27.8 24.9 %all-to-all-done.1 = bf16[16,64,1024]{2,1,0:T(8,128)(2,1)S(1)} async-done(((bf16[16,64,1024]{2,1,0:T(8,128)(2,1)}), bf16[16,64,1024]{2,1,0:T(8,128)(2,1)S(1)}, u32[]{:S(2)}, u32[]{:S(2)}) %all-to-all-start.1) | async-done | bytes 2097184 | tf_op jit(solution)/shard_map/all_to_all | solution.py:45
  52.7 1.3 %fusion.7 = f32[2,64,1024]{2,0,1:T(2,128)S(1)} fusion(bf16[2,16,1]{1,0,2:T(2,128)(2,1)S(1)} %fusion.9, bf16[16,64,1024]{2,1,0:T(8,128)(2,1)S(1)} %all-to-all-done.1), kind=kOutput, calls=%fused_computation.10 | convolution fusion | flops 4194304 | bytes 2621504 | tf_op jit(solution)/shard_map/ks,sxd->kxd/dot_general | solution.py:60
  54.0 1.0 copy.35
  55.0 0.0 all-gather.2.cloned.1.call-update
  55.7 0.0 copy-done.4
  55.7 0.6 dynamic-slice
  57.0 0.1 select_reduce_fusion.2
  57.1 0.2 dynamic-update-slice.1
  57.4 0.1 add_dynamic-update-slice_fusion
  57.5 18.8 %all-reduce.2 = (f32[16]{0:T(128)S(1)}, f32[16]{0:T(128)S(1)}) all-reduce(f32[16]{0:T(128)S(1)} %add_dynamic-update-slice_fusion, f32[16]{0:T(128)S(1)} %dynamic-update-slice.1), channel_id=1, replica_groups=mesh['dp'=8,'table'=16] {'dp'}, use_global_device_ids=true, to_apply=%add | all-reduce | flops 32 | bytes 256
  76.2 0.1 select_reduce_fusion
  76.4 0.1 broadcast_in_dim.13
  76.4 0.1 gt.31
  76.5 15.0 %all-gather.2.cloned.1.call-done = f32[16,64,1024]{2,1,0:T(8,128)} async-done(((f32[2,64,1024]{2,1,0:T(8,128)}), f32[16,64,1024]{2,1,0:T(8,128)}) %all-gather.2.cloned.1.call-update) | async-done | bytes 4194320 | tf_op jit(solution)/shard_map/all_gather | solution.py:65
  91.5 6.6 %fusion.2 = f32[16,64,1024]{2,0,1:T(8,128)S(1)} fusion(f32[16,64,1024]{2,1,0:T(8,128)} %all-gather.2.cloned.1.call-done, f32[16]{0:T(128)S(1)} %get-tuple-element.7), kind=kOutput, calls=%fused_computation.4 | convolution fusion | flops 201326848 | bytes 8388672 | tf_op jit(solution)/shard_map/bk,kxd->bxd/dot_general | solution.py:70
  98.1 0.0 copy-start.1
  98.1 0.0 copy-start.2
  98.1 2.4 %copy.37 = f32[16,64,1024]{2,1,0:T(8,128)S(1)} copy(f32[16,64,1024]{2,0,1:T(8,128)S(1)} %fusion.2) | data formatting | bytes 8388608 | tf_op jit(solution)/shard_map/bk,kxd->bxd/dot_general | solution.py:70
  100.5 0.0 copy-done.1
  100.5 1.0 copy-done.2
  101.5 0.0 copy-start.3
  101.5 4.7 %fusion.5 = (f32[1024,1024]{1,0:T(8,128)}, f32[1024,1024]{1,0:T(8,128)}) fusion(f32[1024,1024]{1,0:T(8,128)S(1)} %copy-done.1, f32[16,64,1024]{2,1,0:T(8,128)S(1)} %copy.37, pred[1024]{0:T(1024)(128)(4,1)S(1)} %gt.31, f32[1024,1024]{1,0:T(8,128)S(1)} %copy-done.2), kind=kLoop, calls=%fused_computation.8 | loop fusion | flops 9437184 | bytes 20972544 | tf_op jit(solution)/shard_map/jit(_where)/select_n | solution.py:23
  106.3 0.0 copy-done.3
  106.3 5.2 %fusion.6 = bf16[1024,1024]{1,0:T(8,128)(2,1)} fusion(bf16[1024,1024]{1,0:T(8,128)(2,1)S(1)} %copy-done.3, f32[1024,1024]{1,0:T(8,128)S(1)} %copy-done.1, f32[16,64,1024]{2,1,0:T(8,128)S(1)} %copy.37, f32[1024,1024]{1,0:T(8,128)S(1)} %copy-done.2, f32[]{:T(128)} %bitcast.16, f32[]{:T(128)} %bitcast.15, pred[1024]{0:T(1024)(128)(4,1)S(1)} %gt.31), kind=kLoop, calls=%fused_computation.9 | loop fusion | flops 16777216 | bytes 16778248 | tf_op jit(solution)/shard_map/jit(_where)/select_n | solution.py:21
  (10 shorter events, 0.1 us)
Async XLA Ops:
  7.2 9.8 %copy-start = (bf16[8,64,1024]{2,1,0:T(8,128)(2,1)S(1)}, bf16[8,64,1024]{2,1,0:T(8,128)(2,1)}, u32[]{:S(2)}) copy-start(bf16[8,64,1024]{2,1,0:T(8,128)(2,1)} %param.10) | copy-start | bytes 3145732
  9.4 13.9 %all-to-all-start = ((s32[16,1,2]{2,1,0:T(1,128)}), s32[16,1,2]{2,1,0:T(1,128)S(1)}, u32[]{:S(2)}, u32[]{:S(2)}) async-start(s32[16,1,2]{2,1,0:T(1,128)} %copy.29), calls=%async_computation | async-start | bytes 16384 | tf_op jit(solution)/shard_map/all_to_all | solution.py:46
  20.4 35.3 %copy-start.4 = (u32[128]{0:T(128)S(1)}, u32[128]{0:T(128)}, u32[]{:S(2)}) copy-start(u32[128]{0:T(128)} %constant.75) | copy-start | bytes 1540
  23.3 29.4 %all-to-all-start.1 = ((bf16[16,64,1024]{2,1,0:T(8,128)(2,1)}), bf16[16,64,1024]{2,1,0:T(8,128)(2,1)S(1)}, u32[]{:S(2)}, u32[]{:S(2)}) async-start(bf16[16,64,1024]{2,1,0:T(8,128)(2,1)} %copy.33), calls=%async_computation.1 | async-start | bytes 4194304 | tf_op jit(solution)/shard_map/all_to_all | solution.py:45
  27.2 64.3 %all-gather.2.cloned.1.call-start = ((), (), s32[]{:S(2)}) async-start(), calls=%async_computation.2 | async-start | bytes 4718592 | tf_op jit(solution)/shard_map/all_gather | solution.py:65
  98.1 2.5 %copy-start.1 = (f32[1024,1024]{1,0:T(8,128)S(1)}, f32[1024,1024]{1,0:T(8,128)}, u32[]{:S(2)}) copy-start(f32[1024,1024]{1,0:T(8,128)} %param.9) | copy-start | bytes 12582916
  98.1 3.5 %copy-start.2 = (f32[1024,1024]{1,0:T(8,128)S(1)}, f32[1024,1024]{1,0:T(8,128)}, u32[]{:S(2)}) copy-start(f32[1024,1024]{1,0:T(8,128)} %param.8) | copy-start | bytes 12582916
  101.5 4.7 %copy-start.3 = (bf16[1024,1024]{1,0:T(8,128)(2,1)S(1)}, bf16[1024,1024]{1,0:T(8,128)(2,1)}, u32[]{:S(2)}) copy-start(bf16[1024,1024]{1,0:T(8,128)(2,1)} %param.7) | copy-start | bytes 6291460
Sparse Core Ops, SparseCore 0:
  55.1 36.3 all-gather.1
where the time goes:
time: 119 us; the launch traced here: 118 us
  waiting for transfers between devices  42.8 us (36%)
  blocking collectives  18.8 us (16%)
  between operations  16.3 us (14%)
  starting transfers between devices  11.5 us (10%)
  other arithmetic  11.4 us (10%)
  matrix products  8.89 us (7%)
  local copies, waits for them, and re-layouts  8.73 us (7%)
    all_to_all x1, waiting for transfers between devices, per_device(): lax.all_to_all(outgoing, 'table', split_axis=0, concat_axis=0, tiled=True)  24.9 us
    unnamed x1, blocking collectives  18.8 us
    all_gather x1, waiting for transfers between devices, per_device(): lax.all_gather(packed, 'dp', axis=0, tiled=True)  15 us
    all_to_all x1, starting transfers between devices, per_device(): lax.all_to_all(labels, 'table', split_axis=0, concat_axis=0, tiled=True)  7.58 us
    dot_general x1, matrix products, per_device(): jnp.einsum('bk,kxd->bxd', placing, all_packed, precision=lax.Precision.HI...  6.56 us
    select_n x1, other arithmetic, adam_rows(): new_values = jnp.where(touched, moved.astype(jnp.bfloat16), values)  5.21 us
    select_n x1, other arithmetic, adam_rows(): new_second = jnp.where(touched, second_next, second_moment)  4.72 us
    all_to_all x1, starting transfers between devices, per_device(): lax.all_to_all(outgoing, 'table', split_axis=0, concat_axis=0, tiled=True)  3.86 us
  transfers between devices with their start and end apart: 3, of which 3 were waited for; matrix products, arithmetic and copies ran while one was open for 5% of the time, Pallas kernels for 0%

commit v1 on v0

v1 whole, which is shorter than its diff:
```python
import functools

import jax
import jax.numpy as jnp
from jax import lax
from jax.experimental import pallas as pl
from jax.experimental.pallas import tpu as pltpu
from jax.sharding import PartitionSpec as P

MESH = pl.DeviceIdType.MESH
BROWS = 64
SLOTS = 8
NSIDE = 4
NC = 4
RB = BROWS // NC
PLANE = [(dx, dy) for dx in range(4) for dy in range(4) if (dx, dy) != (0, 0)]
NP = len(PLANE)
NREP = 8
NOBLK = 1 << 20


def exchange_kernel(
    ids_ref, cnt_ref, grads_hbm,
    gath, idg,
    grads, stage, inc, lab_out, lab_in,
    ld_sem, lab_ss, lab_rs, a_ss, a_rs, id_ss, id_rs, b_ss, b_rs, f_ss, f_rs, s_ss, s_rs,
):
    dp = lax.axis_index("dp")
    tb = lax.axis_index("table")
    z, core = dp // 2, dp % 2
    x, y = tb // NSIDE, tb % NSIDE
    width = grads.shape[2]

    def plane_peer(i):
        dx, dy = PLANE[i]
        return ((x + dx) % NSIDE) * NSIDE + (y + dy) % NSIDE

    def rep_peer(dz, dc):
        return ((z + dz) % NSIDE) * 2 + (core + dc) % 2

    owners = [plane_peer(i) for i in range(NP)] + [tb]
    dp_peers = [(dz, dc) for dz in range(NSIDE) for dc in range(2) if (dz, dc) != (0, 0)]

    load = pltpu.make_async_copy(grads_hbm, grads, ld_sem)
    load.start()

    barrier = pltpu.get_barrier_semaphore()
    for i in range(NP):
        pl.semaphore_signal(barrier, inc=1, device_id=(dp, owners[i]), device_id_type=MESH)
    for dz, dc in dp_peers:
        pl.semaphore_signal(barrier, inc=1, device_id=(rep_peer(dz, dc), tb), device_id_type=MESH)

    count = cnt_ref[0]
    named = [jnp.where(s < count, ids_ref[0, s], NOBLK) for s in range(SLOTS)]
    slot_of = []
    for i in range(NP + 1):
        slot = jnp.int32(0)
        label = jnp.int32(-1)
        for s in range(SLOTS):
            here = (named[s] >> 4) == owners[i]
            slot = jnp.where(here, s, slot)
            label = jnp.where(here, named[s] & 15, label)
        slot_of.append(slot)
        row = jnp.full((1, width), label, jnp.int32)
        if i < NP:
            lab_out[i] = row
        else:
            lab_in[i] = row

    pl.semaphore_wait(barrier, NP + len(dp_peers))

    def label_copy(i):
        return pltpu.make_async_remote_copy(
            src_ref=lab_out.at[i], dst_ref=lab_in.at[i], send_sem=lab_ss.at[i], recv_sem=lab_rs.at[i],
            device_id=(dp, owners[i]), device_id_type=MESH)

    def block_copy(c, i):
        return pltpu.make_async_remote_copy(
            src_ref=stage.at[c, i], dst_ref=inc.at[c, i], send_sem=a_ss.at[c, i], recv_sem=a_rs.at[c, i],
            device_id=(dp, owners[i]), device_id_type=MESH)

    for i in range(NP):
        label_copy(i).start()
    load.wait()

    @pl.loop(0, NC)
    def _(c):
        rows = pl.ds(pl.multiple_of(c * RB, RB), RB)
        for i in range(NP):
            stage[c, i] = grads[slot_of[i], rows, :]
            block_copy(c, i).start()
        inc[c, NP] = grads[slot_of[NP], rows, :]

    for i in range(NP):
        label_copy(i).wait()
    low = jnp.full((1, width), NOBLK, jnp.int32)
    high = jnp.full((1, width), -1, jnp.int32)
    for i in range(NP + 1):
        lab = lab_in[i]
        low = jnp.minimum(low, jnp.where(lab < 0, NOBLK, lab))
        high = jnp.maximum(high, lab)
    two = high > low
    idg[dp, 0:1] = jnp.where(low < NOBLK, low, -1)[:, :128]
    idg[dp, 1:2] = jnp.where(two, high, -1)[:, :128]

    def id_copy(j):
        dz, dc = dp_peers[j]
        return pltpu.make_async_remote_copy(
            src_ref=idg.at[dp], dst_ref=idg.at[dp], send_sem=id_ss.at[j], recv_sem=id_rs.at[j],
            device_id=(rep_peer(dz, dc), tb), device_id_type=MESH)

    for j in range(len(dp_peers)):
        id_copy(j).start()

    def ring_copy(c, j):
        return pltpu.make_async_remote_copy(
            src_ref=gath.at[c, dp], dst_ref=gath.at[c, dp], send_sem=b_ss.at[c, j], recv_sem=b_rs.at[c, j],
            device_id=(rep_peer(1 if j == 0 else 3, 0), tb), device_id_type=MESH)

    def forward_copy(c, j):
        origin = rep_peer(3 if j == 0 else 1, 0)
        return pltpu.make_async_remote_copy(
            src_ref=gath.at[c, origin, j], dst_ref=gath.at[c, origin, j], send_sem=f_ss.at[c, j], recv_sem=f_rs.at[c, j],
            device_id=(rep_peer(1 if j == 0 else 3, 0), tb), device_id_type=MESH)

    def core_copy(c, dz):
        origin = rep_peer(dz, 0)
        return pltpu.make_async_remote_copy(
            src_ref=gath.at[c, origin], dst_ref=gath.at[c, origin], send_sem=s_ss.at[c, dz], recv_sem=s_rs.at[c, dz],
            device_id=(rep_peer(0, 1), tb), device_id_type=MESH)

    def second_hop(c):
        for j in range(2):
            ring_copy(c, j).wait_recv()
            forward_copy(c, j).start()
            core_copy(c, 3 if j == 0 else 1).start()

    def third_hop(c):
        for j in range(2):
            forward_copy(c, j).wait_recv()
        core_copy(c, 2).start()

    @pl.loop(0, NC)
    def _(c):
        for i in range(NP):
            block_copy(c, i).wait_recv()
        sum_low = jnp.zeros((RB, width), jnp.float32)
        sum_high = jnp.zeros((RB, width), jnp.float32)
        for i in range(NP + 1):
            lab = lab_in[i]
            block = inc[c, i].astype(jnp.float32)
            sum_low += jnp.where(lab == low, 1.0, 0.0) * block
            sum_high += jnp.where((lab == high) & two, 1.0, 0.0) * block
        gath[c, dp, 0] = sum_low
        gath[c, dp, 1] = sum_high
        for j in range(2):
            ring_copy(c, j).start()
        core_copy(c, 0).start()

        @pl.when(c >= 1)
        def _():
            second_hop(c - 1)

        @pl.when(c >= 2)
        def _():
            third_hop(c - 2)

    third_hop(NC - 2)
    second_hop(NC - 1)
    third_hop(NC - 1)

    for j in range(len(dp_peers)):
        id_copy(j).wait()

    @pl.loop(0, NC)
    def _(c):
        for dz in range(NSIDE):
            core_copy(c, dz).wait()
        for j in range(2):
            ring_copy(c, j).wait_send()
            forward_copy(c, j).wait_send()
        for i in range(NP):
            block_copy(c, i).wait_send()


def adam_kernel(
    ids_ref, scale_ref, gath, values, first, second,
    out_v, out_f, out_s,
    grad, new_v, new_f, new_s, hit, sem,
):
    nblk = grad.shape[0]
    for b in range(nblk):
        hit[b] = 0
    for r in range(NREP):
        for k in range(2):
            b = ids_ref[r, k, 0]

            @pl.when(b >= 0)
            def _():
                @pl.when(hit[b] == 0)
                def _():
                    for c in range(NC):
                        grad[b, c] = gath[c, r, k]

                @pl.when(hit[b] > 0)
                def _():
                    for c in range(NC):
                        grad[b, c] += gath[c, r, k]

                hit[b] = 1

    inv_one = scale_ref[0]
    inv_two = scale_ref[1]

    def copies(b, v, f, s):
        rows = pl.ds(pl.multiple_of(b * BROWS, BROWS), BROWS)
        return [
            pltpu.make_async_copy(v.at[rows], out_v.at[rows], sem.at[0, b]),
            pltpu.make_async_copy(f.at[rows], out_f.at[rows], sem.at[1, b]),
            pltpu.make_async_copy(s.at[rows], out_s.at[rows], sem.at[2, b]),
        ]

    @pl.loop(0, nblk)
    def _(b):
        @pl.when(hit[b] > 0)
        def _():
            for c in range(NC):
                rows = pl.ds(pl.multiple_of(b * BROWS + c * RB, RB), RB)
                g = grad[b, c]
                f = 0.9 * first[rows, :] + (1.0 - 0.9) * g
                s = 0.99 * second[rows, :] + (1.0 - 0.99) * g * g
                new_f[rows, :] = f
                new_s[rows, :] = s
                moved = values[rows, :].astype(jnp.float32) - 0.05 * (f / inv_one) / (jnp.sqrt(s / inv_two) + 1e-08)
                new_v[rows, :] = moved.astype(jnp.bfloat16)
            for cp in copies(b, new_v, new_f, new_s):
                cp.start()

        @pl.when(hit[b] == 0)
        def _():
            for cp in copies(b, values, first, second):
                cp.start()

    @pl.loop(0, nblk)
    def _(b):
        for cp in copies(b, new_v, new_f, new_s):
            cp.wait()


def per_device(values, first_moment, second_moment, grads, block_ids, live_counts, step_count):
    own_rows, width = values.shape
    nblk = own_rows // BROWS
    dma = pltpu.SemaphoreType.DMA
    vmem = pl.BlockSpec(memory_space=pltpu.VMEM)
    smem = pl.BlockSpec(memory_space=pltpu.SMEM)
    hbm = pl.BlockSpec(memory_space=pl.ANY)
    gath, ids = pl.pallas_call(
        exchange_kernel,
        out_shape=(
            jax.ShapeDtypeStruct((NC, NREP, 2, RB, width), jnp.float32),
            jax.ShapeDtypeStruct((NREP, 2, 128), jnp.int32),
        ),
        in_specs=[smem, smem, hbm],
        out_specs=(vmem, vmem),
        scratch_shapes=[
            pltpu.VMEM((SLOTS, BROWS, width), jnp.bfloat16),
            pltpu.VMEM((NC, NP, RB, width), jnp.bfloat16),
            pltpu.VMEM((NC, NP + 1, RB, width), jnp.bfloat16),
            pltpu.VMEM((NP, 1, width), jnp.int32),
            pltpu.VMEM((NP + 1, 1, width), jnp.int32),
            dma(()), dma((NP,)), dma((NP,)), dma((NC, NP)), dma((NC, NP)),
            dma((NREP - 1,)), dma((NREP - 1,)), dma((NC, 2)), dma((NC, 2)),
            dma((NC, 2)), dma((NC, 2)), dma((NC, NSIDE)), dma((NC, NSIDE)),
        ],
        compiler_params=pltpu.CompilerParams(
            collective_id=0, has_side_effects=True, vmem_limit_bytes=24 << 20),
        name="exchange",
    )(block_ids, live_counts, grads)
    steps = step_count[0].astype(jnp.float32)
    scales = jnp.stack([1.0 - jnp.power(jnp.float32(0.9), steps), 1.0 - jnp.power(jnp.float32(0.99), steps)])
    return pl.pallas_call(
        adam_kernel,
        out_shape=tuple(jax.ShapeDtypeStruct(a.shape, a.dtype) for a in (values, first_moment, second_moment)),
        in_specs=[smem, smem, vmem, vmem, vmem, vmem],
        out_specs=(hbm, hbm, hbm),
        scratch_shapes=[
            pltpu.VMEM((nblk, NC, RB, width), jnp.float32),
            pltpu.VMEM((own_rows, width), jnp.bfloat16),
            pltpu.VMEM((own_rows, width), jnp.float32),
            pltpu.VMEM((own_rows, width), jnp.float32),
            pltpu.SMEM((nblk,), jnp.int32),
            dma((3, nblk)),
        ],
        compiler_params=pltpu.CompilerParams(vmem_limit_bytes=40 << 20),
        name="adam",
    )(ids, scales, gath, values, first_moment, second_moment)


def solution(mesh):
    in_specs = (
        P("table", None),
        P("table", None),
        P("table", None),
        P(("dp", "table"), None, None),
        P(("dp", "table"), None),
        P(("dp", "table")),
        P(),
    )
    out_specs = (P("table", None), P("table", None), P("table", None))
    return jax.shard_map(
        per_device, mesh=mesh, in_specs=in_specs, out_specs=out_specs, check_vma=False
    )
```

time: 119 us -> 64.1 us (0.54)
  Pallas kernels: 0 us -> 56.1 us
  waiting for transfers between devices: 42.8 us -> 0 us
  blocking collectives: 18.8 us -> 0 us
  between operations: 16.3 us -> 2.03 us
  starting transfers between devices: 11.5 us -> 0 us
  other arithmetic: 11.4 us -> 0.08 us
  matrix products: 8.89 us -> 0 us
  local copies, waits for them, and re-layouts: 8.73 us -> 5.65 us
    pallas_call x0 -> x2, Pallas kernels: none -> 56.1 us  [the longest x1 48.7 us: per_device(): pl.pallas_call(exchange_kernel, out_shape=(jax.ShapeDtypeStruct((NC, NREP...]
    all_to_all x2 -> x0, waiting for transfers between devices: 27.8 us -> none  [the longest x1 24.9 us: per_device(): lax.all_to_all(outgoing, 'table', split_axis=0, concat_axis=0, tiled=True)]
    unnamed x1 -> x0, blocking collectives: 18.8 us -> none
    all_gather x1 -> x0, waiting for transfers between devices: 15 us -> none  [per_device(): lax.all_gather(packed, 'dp', axis=0, tiled=True)]
    all_to_all x2 -> x0, starting transfers between devices: 11.4 us -> none  [the longest x1 7.58 us: per_device(): lax.all_to_all(labels, 'table', split_axis=0, concat_axis=0, tiled=True)]
    select_n x2 -> x0, other arithmetic: 9.92 us -> none  [the longest x1 5.21 us: adam_rows(): new_values = jnp.where(touched, moved.astype(jnp.bfloat16), values)]
    dot_general x4 -> x0, matrix products: 8.89 us -> none  [the longest x1 6.56 us: per_device(): jnp.einsum('bk,kxd->bxd', placing, all_packed, precision=lax.Precision.HI...]
    unnamed x14 -> x8, local copies, waits for them, and re-layouts: 1.86 us -> 5.65 us
  transfers between devices with their start and end apart: 3 -> 0, of which waited for: 3 -> 0; matrix products, arithmetic and copies ran while one was open for 5% -> 0% of each run, Pallas kernels for 0% -> 0%
where the time goes in v1:
time: 64.1 us; the launch traced here: 63.8 us
  Pallas kernels  56.1 us (88%)
  local copies, waits for them, and re-layouts  5.65 us (9%)
  between operations  2.03 us (3%)
    pallas_call x1, Pallas kernels, per_device(): pl.pallas_call(exchange_kernel, out_shape=(jax.ShapeDtypeStruct((NC, NREP...  48.7 us
    pallas_call x1, Pallas kernels, per_device(): pl.pallas_call(adam_kernel, out_shape=tuple((jax.ShapeDtypeStruct(a.shape...  7.38 us
    unnamed x8, local copies, waits for them, and re-layouts  5.65 us

profile of v1, /device:TPU:1, one launch (start us, length us, event | category | flops | bytes accessed | tf_op | source)
XLA Modules:
  0.0 63.8 jit_solution(15954054717814825613)
XLA Ops:
  2.0 0.1 pad_maximum_fusion.scale_ref
  2.1 0.0 copy-start.2
  2.1 1.2 %copy-done.2 = bf16[8,64,1024]{2,1,0:T(8,128)(2,1)S(1)} copy-done((bf16[8,64,1024]{2,1,0:T(8,128)(2,1)S(1)}, bf16[8,64,1024]{2,1,0:T(8,128)(2,1)}, u32[]{:S(2)}) %copy-start.2) | copy-done | bytes 1048600
  3.3 0.0 copy-start.3
  3.3 0.7 %copy-done.3 = s32[1,8]{1,0:T(1,128)S(1)} copy-done((s32[1,8]{1,0:T(1,128)S(1)}, s32[1,8]{1,0:T(1,128)}, u32[]{:S(2)}) %copy-start.3) | copy-done | bytes 56
  4.0 48.7 %exchange.1 = (f32[4,8,2,16,1024]{4,3,2,1,0:T(8,128)S(1)}, s32[8,2,128]{2,1,0:T(2,128)S(1)}) custom-call(s32[1,8]{1,0:T(1,128)S(1)} %copy-done.3, s32[1]{0:T(128)S(6)} %copy.10.cnt_ref, bf16[8,64,1024]{2,1,0:T(8,128)(2,1)S(1)} %copy-done.2), custom_call_target="tpu_custom_call" | custom-call | tf_op jit(solution)/shard_map/exchange/pallas_call | solution.py:257
  52.7 0.0 copy-start
  52.7 2.2 %copy-done = f32[1024,1024]{1,0:T(8,128)S(1)} copy-done((f32[1024,1024]{1,0:T(8,128)S(1)}, f32[1024,1024]{1,0:T(8,128)}, u32[]{:S(2)}) %copy-start) | copy-done | bytes 4194328
  54.9 0.0 copy-start.1
  54.9 1.6 %copy-done.1 = bf16[1024,1024]{1,0:T(8,128)(2,1)S(1)} copy-done((bf16[1024,1024]{1,0:T(8,128)(2,1)S(1)}, bf16[1024,1024]{1,0:T(8,128)(2,1)}, u32[]{:S(2)}) %copy-start.1) | copy-done | bytes 2097176
  56.5 7.4 %adam.1 = (bf16[1024,1024]{1,0:T(8,128)(2,1)}, f32[1024,1024]{1,0:T(8,128)}, f32[1024,1024]{1,0:T(8,128)}) custom-call(s32[8,2,128]{2,1,0:T(2,128)S(1)} %get-tuple-element.5.ids_ref, f32[2]{0:T(128)S(1)} %pad_maximum_fusion.scale_ref, f32[4,8,2,16,1024]{4,3,2,1,0:T(8,128)S(1)} %get-tuple-element.6.gath, bf16[1024,1024]{1,0:T(8,128)(2,1)S(1)} %copy-done.1, ...), custom_call_target="tpu_custom_call" | custom-call | tf_op jit(solution)/shard_map/adam/pallas_call | solution.py:281
Async XLA Ops:
  2.1 1.2 %copy-start.2 = (bf16[8,64,1024]{2,1,0:T(8,128)(2,1)S(1)}, bf16[8,64,1024]{2,1,0:T(8,128)(2,1)}, u32[]{:S(2)}) copy-start(bf16[8,64,1024]{2,1,0:T(8,128)(2,1)} %grads_hbm.1) | copy-start | bytes 3145732
  3.3 0.7 %copy-start.3 = (s32[1,8]{1,0:T(1,128)S(1)}, s32[1,8]{1,0:T(1,128)}, u32[]{:S(2)}) copy-start(s32[1,8]{1,0:T(1,128)} %ids_ref.1) | copy-start | bytes 100
  52.7 2.2 %copy-start = (f32[1024,1024]{1,0:T(8,128)S(1)}, f32[1024,1024]{1,0:T(8,128)}, u32[]{:S(2)}) copy-start(f32[1024,1024]{1,0:T(8,128)} %first.1) | copy-start | bytes 12582916
  54.9 1.6 %copy-start.1 = (bf16[1024,1024]{1,0:T(8,128)(2,1)S(1)}, bf16[1024,1024]{1,0:T(8,128)(2,1)}, u32[]{:S(2)}) copy-start(bf16[1024,1024]{1,0:T(8,128)(2,1)} %values.1) | copy-start | bytes 6291460

commit v2 on v1

v2 whole, which is shorter than its diff:
```python
import jax
import jax.numpy as jnp
from jax import lax
from jax.experimental import pallas as pl
from jax.experimental.pallas import tpu as pltpu
from jax.sharding import PartitionSpec as P

MESH = pl.DeviceIdType.MESH
BROWS = 64
SLOTS = 8
NSIDE = 4
NC = 4
RB = BROWS // NC
PLANE = [(1, 2), (0, 1), (1, 1), (0, 2), (3, 2), (0, 3), (3, 3), (2, 0), (2, 1), (1, 0), (1, 3), (2, 2), (2, 3), (3, 0), (3, 1)]
NP = len(PLANE)
NREP = 8
NOBLK = 1 << 20


def exchange_kernel(
    cnt_ref, step_ref, ids_hbm, grads_hbm, values_hbm, first_hbm, second_hbm,
    gath, idg, values, first, second,
    ids_ref, grads, stage, inc, lab_out, lab_in,
    sm_sem, ld_sem, lab_ss, lab_rs, a_ss, a_rs, id_ss, id_rs, b_ss, b_rs, s_ss, s_rs,
):
    dp = lax.axis_index("dp")
    tb = lax.axis_index("table")
    z, core = dp // 2, dp % 2
    x, y = tb // NSIDE, tb % NSIDE
    width = grads.shape[2]

    def plane_peer(i):
        dx, dy = PLANE[i]
        return ((x + dx) % NSIDE) * NSIDE + (y + dy) % NSIDE

    def rep_peer(dz, dc):
        return ((z + dz) % NSIDE) * 2 + (core + dc) % 2

    owners = [plane_peer(i) for i in range(NP)] + [tb]
    dp_peers = [(dz, dc) for dz in range(NSIDE) for dc in range(2) if (dz, dc) != (0, 0)]

    small = [
        pltpu.make_async_copy(ids_hbm, ids_ref, sm_sem.at[0]),
    ]
    load = pltpu.make_async_copy(grads_hbm, grads, ld_sem.at[0])
    held = [
        pltpu.make_async_copy(values_hbm, values, ld_sem.at[1]),
        pltpu.make_async_copy(first_hbm, first, ld_sem.at[2]),
        pltpu.make_async_copy(second_hbm, second, ld_sem.at[3]),
    ]
    for cp in small:
        cp.start()
    load.start()

    barrier = pltpu.get_barrier_semaphore()
    for i in range(NP):
        pl.semaphore_signal(barrier, inc=1, device_id=(dp, owners[i]), device_id_type=MESH)
    for dz, dc in dp_peers:
        pl.semaphore_signal(barrier, inc=1, device_id=(rep_peer(dz, dc), tb), device_id_type=MESH)

    for cp in small:
        cp.wait()
    count = cnt_ref[0]
    named = [jnp.where(s < count, ids_ref[0, s], NOBLK) for s in range(SLOTS)]
    slot_of = []
    for i in range(NP + 1):
        slot = jnp.int32(0)
        label = jnp.int32(-1)
        for s in range(SLOTS):
            here = (named[s] >> 4) == owners[i]
            slot = jnp.where(here, s, slot)
            label = jnp.where(here, named[s] & 15, label)
        slot_of.append(slot)
        row = jnp.full((1, width), label, jnp.int32)
        if i < NP:
            lab_out[i] = row
        else:
            lab_in[i] = row

    load.wait()
    pl.semaphore_wait(barrier, NP + len(dp_peers))

    def label_copy(i):
        return pltpu.make_async_remote_copy(
            src_ref=lab_out.at[i], dst_ref=lab_in.at[i], send_sem=lab_ss.at[i], recv_sem=lab_rs.at[i],
            device_id=(dp, owners[i]), device_id_type=MESH)

    def block_copy(c, i):
        return pltpu.make_async_remote_copy(
            src_ref=stage.at[c, i], dst_ref=inc.at[c, i], send_sem=a_ss.at[c], recv_sem=a_rs.at[c],
            device_id=(dp, owners[i]), device_id_type=MESH)

    def all_blocks(c):
        blocks = pl.ds(0, NP)
        return pltpu.make_async_remote_copy(
            src_ref=stage.at[c, blocks], dst_ref=inc.at[c, blocks], send_sem=a_ss.at[c], recv_sem=a_rs.at[c],
            device_id=(dp, owners[0]), device_id_type=MESH)

    def send_blocks(c):
        rows = pl.ds(pl.multiple_of(c * RB, RB), RB)
        for i in range(NP):
            stage[c, i] = grads[slot_of[i], rows, :]
            block_copy(c, i).start()
        inc[c, NP] = grads[slot_of[NP], rows, :]

    send_blocks(0)
    for i in range(NP):
        label_copy(i).start()

    @pl.loop(1, NC)
    def _(c):
        send_blocks(c)

    for cp in held:
        cp.start()

    for i in range(NP):
        label_copy(i).wait()
    low = jnp.full((1, width), NOBLK, jnp.int32)
    high = jnp.full((1, width), -1, jnp.int32)
    for i in range(NP + 1):
        lab = lab_in[i]
        low = jnp.minimum(low, jnp.where(lab < 0, NOBLK, lab))
        high = jnp.maximum(high, lab)
    two = high > low
    idg[dp, 0:1] = jnp.where(low < NOBLK, low, -1)[:, :128]
    idg[dp, 1:2] = jnp.where(two, high, -1)[:, :128]
    idg[NREP] = jnp.full((2, 128), step_ref[0], jnp.int32)

    def id_copy(j):
        dz, dc = dp_peers[j]
        return pltpu.make_async_remote_copy(
            src_ref=idg.at[dp], dst_ref=idg.at[dp], send_sem=id_ss.at[j], recv_sem=id_rs.at[j],
            device_id=(rep_peer(dz, dc), tb), device_id_type=MESH)

    for j in range(len(dp_peers)):
        id_copy(j).start()

    def ring_copy(c, dz):
        return pltpu.make_async_remote_copy(
            src_ref=gath.at[c, dp], dst_ref=gath.at[c, dp], send_sem=b_ss.at[c, dz - 1], recv_sem=b_rs.at[c, dz - 1],
            device_id=(rep_peer(dz, 0), tb), device_id_type=MESH)

    def core_copy(c, dz):
        origin = rep_peer(dz, 0)
        return pltpu.make_async_remote_copy(
            src_ref=gath.at[c, origin], dst_ref=gath.at[c, origin], send_sem=s_ss.at[c, dz], recv_sem=s_rs.at[c, dz],
            device_id=(rep_peer(0, 1), tb), device_id_type=MESH)

    def second_hop(c):
        for dz in (1, 3, 2):
            ring_copy(c, dz).wait_recv()
            core_copy(c, NSIDE - dz).start()

    @pl.loop(0, NC)
    def _(c):
        all_blocks(c).wait_recv()
        sum_low = jnp.zeros((RB, width), jnp.float32)
        sum_high = jnp.zeros((RB, width), jnp.float32)
        for i in range(NP + 1):
            lab = lab_in[i]
            block = inc[c, i].astype(jnp.float32)
            sum_low += jnp.where(lab == low, 1.0, 0.0) * block
            sum_high += jnp.where((lab == high) & two, 1.0, 0.0) * block
        gath[c, dp, 0] = sum_low
        gath[c, dp, 1] = sum_high
        for dz in (1, 3, 2):
            ring_copy(c, dz).start()
        core_copy(c, 0).start()

        @pl.when(c >= 1)
        def _():
            second_hop(c - 1)

    second_hop(NC - 1)

    for j in range(len(dp_peers)):
        id_copy(j).wait()
    for cp in held:
        cp.wait()

    @pl.loop(0, NC)
    def _(c):
        for dz in range(NSIDE):
            core_copy(c, dz).wait()
        for dz in range(1, NSIDE):
            ring_copy(c, dz).wait_send()
        all_blocks(c).wait_send()


def adam_kernel(
    ids_ref, gath, values, first, second,
    out_v, out_f, out_s,
    tmp, new_v, new_f, new_s, count, names, sem,
):
    nblk = values.shape[0] // BROWS
    for b in range(nblk + 1):
        count[b] = 0
    for q in range(2 * NREP):
        named = ids_ref[q // 2, q % 2, 0]
        b = jnp.where(named < 0, nblk, named)
        n = count[b]
        names[b * 2 * NREP + n] = q
        count[b] = n + 1

    steps = ids_ref[NREP, 0, 0]
    power_one, power_two = lax.fori_loop(
        0, steps, lambda _, p: (p[0] * 0.9, p[1] * 0.99), (jnp.float32(1.0), jnp.float32(1.0)))
    one = jnp.full((1, 1024), 1.0 - power_one, jnp.float32)
    two = jnp.full((1, 1024), 1.0 - power_two, jnp.float32)
    rate = 0.05 / one
    scale = 1.0 / two

    def copies(b, v, f, s):
        rows = pl.ds(pl.multiple_of(b * BROWS, BROWS), BROWS)
        return [
            pltpu.make_async_copy(v.at[rows], out_v.at[rows], sem.at[0, b]),
            pltpu.make_async_copy(f.at[rows], out_f.at[rows], sem.at[1, b]),
            pltpu.make_async_copy(s.at[rows], out_s.at[rows], sem.at[2, b]),
        ]

    def update(b, grad_of):
        for c in range(NC):
            rows = pl.ds(pl.multiple_of(b * BROWS + c * RB, RB), RB)
            g = grad_of(c)
            f = 0.9 * first[rows, :] + (1.0 - 0.9) * g
            s = 0.99 * second[rows, :] + (1.0 - 0.99) * g * g
            new_f[rows, :] = f
            new_s[rows, :] = s
            moved = values[rows, :].astype(jnp.float32) - rate * f / (jnp.sqrt(scale * s) + 1e-08)
            new_v[rows, :] = moved.astype(jnp.bfloat16)
        for cp in copies(b, new_v, new_f, new_s):
            cp.start()

    @pl.loop(0, nblk)
    def _(b):
        @pl.when(count[b] == 0)
        def _():
            for cp in copies(b, values, first, second):
                cp.start()

    @pl.loop(0, nblk)
    def _(b):
        n = count[b]
        base = b * 2 * NREP

        def name_of(j):
            q = names[base + j]
            return q >> 1, q & 1

        @pl.when(n == 1)
        def _():
            r, k = name_of(0)
            update(b, lambda c: gath[c, r, k])

        @pl.when(n > 1)
        def _():
            r, k = name_of(0)
            r1, k1 = name_of(1)
            for c in range(NC):
                tmp[c] = gath[c, r, k] + gath[c, r1, k1]

            def more(j, _):
                rj, kj = name_of(j)
                for c in range(NC):
                    tmp[c] += gath[c, rj, kj]
                return 0

            lax.fori_loop(2, n, more, 0)
            update(b, lambda c: tmp[c])

    @pl.loop(0, nblk)
    def _(b):
        for cp in copies(b, new_v, new_f, new_s):
            cp.wait()


def per_device(values, first_moment, second_moment, grads, block_ids, live_counts, step_count):
    own_rows, width = values.shape
    nblk = own_rows // BROWS
    dma = pltpu.SemaphoreType.DMA
    vmem = pl.BlockSpec(memory_space=pltpu.VMEM)
    smem = pl.BlockSpec(memory_space=pltpu.SMEM)
    hbm = pl.BlockSpec(memory_space=pltpu.HBM)
    like = lambda a: jax.ShapeDtypeStruct(a.shape, a.dtype)
    gath, ids, values_in, first_in, second_in = pl.pallas_call(
        exchange_kernel,
        out_shape=(
            jax.ShapeDtypeStruct((NC, NREP, 2, RB, width), jnp.float32),
            jax.ShapeDtypeStruct((NREP + 1, 2, 128), jnp.int32),
            like(values), like(first_moment), like(second_moment),
        ),
        in_specs=[smem, smem] + [hbm] * 5,
        out_specs=(vmem,) * 5,
        scratch_shapes=[
            pltpu.SMEM(block_ids.shape, jnp.int32),
            pltpu.VMEM((SLOTS, BROWS, width), jnp.bfloat16),
            pltpu.VMEM((NC, NP, RB, width), jnp.bfloat16),
            pltpu.VMEM((NC, NP + 1, RB, width), jnp.bfloat16),
            pltpu.VMEM((NP, 1, width), jnp.int32),
            pltpu.VMEM((NP + 1, 1, width), jnp.int32),
            dma((3,)), dma((4,)), dma((NP,)), dma((NP,)), dma((NC,)), dma((NC,)),
            dma((NREP - 1,)), dma((NREP - 1,)), dma((NC, NSIDE - 1)), dma((NC, NSIDE - 1)),
            dma((NC, NSIDE)), dma((NC, NSIDE)),
        ],
        compiler_params=pltpu.CompilerParams(
            collective_id=0, has_side_effects=True, vmem_limit_bytes=24 << 20),
        name="exchange",
    )(live_counts, step_count, *[pltpu.with_memory_space_constraint(a, pltpu.HBM) for a in (block_ids, grads, values, first_moment, second_moment)])
    return pl.pallas_call(
        adam_kernel,
        out_shape=(like(values), like(first_moment), like(second_moment)),
        in_specs=[smem, vmem, vmem, vmem, vmem],
        out_specs=(hbm, hbm, hbm),
        scratch_shapes=[
            pltpu.VMEM((NC, RB, width), jnp.float32),
            pltpu.VMEM((own_rows, width), jnp.bfloat16),
            pltpu.VMEM((own_rows, width), jnp.float32),
            pltpu.VMEM((own_rows, width), jnp.float32),
            pltpu.SMEM((nblk + 1,), jnp.int32),
            pltpu.SMEM(((nblk + 1) * 2 * NREP,), jnp.int32),
            dma((3, nblk)),
        ],
        compiler_params=pltpu.CompilerParams(vmem_limit_bytes=24 << 20),
        name="adam",
    )(ids, gath, values_in, first_in, second_in)


def solution(mesh):
    in_specs = (
        P("table", None),
        P("table", None),
        P("table", None),
        P(("dp", "table"), None, None),
        P(("dp", "table"), None),
        P(("dp", "table")),
        P(),
    )
    out_specs = (P("table", None), P("table", None), P("table", None))
    return jax.shard_map(
        per_device, mesh=mesh, in_specs=in_specs, out_specs=out_specs, check_vma=False
    )
```

time: 64.1 us -> 52.6 us (0.82)
  Pallas kernels: 56.1 us -> 50.4 us
  local copies, waits for them, and re-layouts: 5.65 us -> 0 us
    unnamed x8 -> x0, local copies, waits for them, and re-layouts: 5.65 us -> none
    pallas_call x1, Pallas kernels: 48.7 us -> 45.2 us  [per_device(): pl.pallas_call(exchange_kernel, out_shape=(jax.ShapeDtypeStruct((NC, NREP...]
    pallas_call x1, Pallas kernels: 7.38 us -> 5.17 us  [per_device(): pl.pallas_call(adam_kernel, out_shape=(like(values), like(first_moment),...]
where the time goes in v2:
time: 52.6 us; the launch traced here: 52.3 us
  Pallas kernels  50.4 us (96%)
  between operations  1.93 us (4%)
    pallas_call x1, Pallas kernels, per_device(): pl.pallas_call(exchange_kernel, out_shape=(jax.ShapeDtypeStruct((NC, NREP...  45.2 us
    pallas_call x1, Pallas kernels, per_device(): pl.pallas_call(adam_kernel, out_shape=(like(values), like(first_moment),...  5.17 us

profile of v2, /device:TPU:1, one launch (start us, length us, event | category | flops | bytes accessed | tf_op | source)
XLA Modules:
  0.0 52.3 jit_solution(2388341015275309964)
XLA Ops:
  1.9 45.2 %exchange.1 = (f32[4,8,2,16,1024]{4,3,2,1,0:T(8,128)S(1)}, s32[9,2,128]{2,1,0:T(2,128)S(1)}, bf16[1024,1024]{1,0:T(8,128)(2,1)S(1)}, f32[1024,1024]{1,0:T(8,128)S(1)}, f32[1024,1024]{1,0:T(8,128)S(1)}) custom-call(s32[1]{0:T(128)S(6)} %copy.10.cnt_ref, s32[1]{0:T(128)S(6)} %copy.11.step_ref, s32[1,8]{1,0:T(1,128)} %ids_hbm.1, ...), custom_call_target="tpu_custom_call" | custom-call | tf_op jit(solution)/shard_map/exchange/pallas_call | solution.py:286
  47.2 5.2 %adam.1 = (bf16[1024,1024]{1,0:T(8,128)(2,1)}, f32[1024,1024]{1,0:T(8,128)}, f32[1024,1024]{1,0:T(8,128)}) custom-call(s32[9,2,128]{2,1,0:T(2,128)S(1)} %get-tuple-element.8.ids_ref, f32[4,8,2,16,1024]{4,3,2,1,0:T(8,128)S(1)} %get-tuple-element.9.gath, bf16[1024,1024]{1,0:T(8,128)(2,1)S(1)} %get-tuple-element.10.values, ...), custom_call_target="tpu_custom_call" | custom-call | tf_op jit(solution)/shard_map/adam/pallas_call | solution.py:310

commit v3 on v2

--- a/solution.py
+++ b/solution.py
@@ -9,25 +9,29 @@
 BROWS = 64
 SLOTS = 8
 NSIDE = 4
-NC = 4
-RB = BROWS // NC
-PLANE = [(1, 2), (0, 1), (1, 1), (0, 2), (3, 2), (0, 3), (3, 3), (2, 0), (2, 1), (1, 0), (1, 3), (2, 2), (2, 3), (3, 0), (3, 1)]
+RB = 16
+CW = 256
+NROW = BROWS // RB
+NCOL = 1024 // CW
+NC = NROW * NCOL
+PLANE = [(2, 2), (1, 2), (3, 2), (2, 1), (2, 3), (1, 1), (3, 3), (1, 3), (3, 1), (0, 2), (2, 0), (0, 1), (0, 3), (1, 0), (3, 0)]
 NP = len(PLANE)
 NREP = 8
+LAST = (4, 3, 2, 5, 1, 6, 0)
+LAG = 5
 NOBLK = 1 << 20
 
 
 def exchange_kernel(
     cnt_ref, step_ref, ids_hbm, grads_hbm, values_hbm, first_hbm, second_hbm,
     gath, idg, values, first, second,
-    ids_ref, grads, stage, inc, lab_out, lab_in,
-    sm_sem, ld_sem, lab_ss, lab_rs, a_ss, a_rs, id_ss, id_rs, b_ss, b_rs, s_ss, s_rs,
+    ids_ref, grads, stage, inc, lab_out, lab_in, weight,
+    sm_sem, ld_sem, lab_ss, lab_rs, a_ss, a_rs, id_ss, id_rs, b_ss, b_rs, s_ss, s_rs, l_ss, l_rs,
 ):
     dp = lax.axis_index("dp")
     tb = lax.axis_index("table")
     z, core = dp // 2, dp % 2
     x, y = tb // NSIDE, tb % NSIDE
-    width = grads.shape[2]
 
     def plane_peer(i):
         dx, dy = PLANE[i]
@@ -71,7 +75,7 @@
             slot = jnp.where(here, s, slot)
             label = jnp.where(here, named[s] & 15, label)
         slot_of.append(slot)
-        row = jnp.full((1, width), label, jnp.int32)
+        row = jnp.full((1, CW), label, jnp.int32)
         if i < NP:
             lab_out[i] = row
         else:
@@ -82,26 +86,27 @@
 
     def label_copy(i):
         return pltpu.make_async_remote_copy(
-            src_ref=lab_out.at[i], dst_ref=lab_in.at[i], send_sem=lab_ss.at[i], recv_sem=lab_rs.at[i],
+            src_ref=lab_out.at[i], dst_ref=lab_in.at[i], send_sem=lab_ss, recv_sem=lab_rs,
             device_id=(dp, owners[i]), device_id_type=MESH)
 
     def block_copy(c, i):
         return pltpu.make_async_remote_copy(
-            src_ref=stage.at[c, i], dst_ref=inc.at[c, i], send_sem=a_ss.at[c], recv_sem=a_rs.at[c],
+            src_ref=stage.at[c, i], dst_ref=inc.at[c, i], send_sem=a_ss, recv_sem=a_rs.at[c],
             device_id=(dp, owners[i]), device_id_type=MESH)
 
     def all_blocks(c):
         blocks = pl.ds(0, NP)
         return pltpu.make_async_remote_copy(
-            src_ref=stage.at[c, blocks], dst_ref=inc.at[c, blocks], send_sem=a_ss.at[c], recv_sem=a_rs.at[c],
+            src_ref=stage.at[c, blocks], dst_ref=inc.at[c, blocks], send_sem=a_ss, recv_sem=a_rs.at[c],
             device_id=(dp, owners[0]), device_id_type=MESH)
 
     def send_blocks(c):
-        rows = pl.ds(pl.multiple_of(c * RB, RB), RB)
+        rows = pl.ds(pl.multiple_of((c // NCOL) * RB, RB), RB)
+        cols = pl.ds(pl.multiple_of((c % NCOL) * CW, CW), CW)
         for i in range(NP):
-            stage[c, i] = grads[slot_of[i], rows, :]
+            stage[c, i] = grads[slot_of[i], rows, cols]
             block_copy(c, i).start()
-        inc[c, NP] = grads[slot_of[NP], rows, :]
+        inc[c, NP] = grads[slot_of[NP], rows, cols]
 
     send_blocks(0)
     for i in range(NP):
@@ -114,15 +119,20 @@
     for cp in held:
         cp.start()
 
-    for i in range(NP):
-        label_copy(i).wait()
-    low = jnp.full((1, width), NOBLK, jnp.int32)
-    high = jnp.full((1, width), -1, jnp.int32)
+    pltpu.make_async_remote_copy(
+        src_ref=lab_out, dst_ref=lab_in.at[pl.ds(0, NP)], send_sem=lab_ss, recv_sem=lab_rs,
+        device_id=(dp, owners[0]), device_id_type=MESH).wait()
+    low = jnp.full((1, CW), NOBLK, jnp.int32)
+    high = jnp.full((1, CW), -1, jnp.int32)
     for i in range(NP + 1):
         lab = lab_in[i]
         low = jnp.minimum(low, jnp.where(lab < 0, NOBLK, lab))
         high = jnp.maximum(high, lab)
     two = high > low
+    for i in range(NP + 1):
+        lab = lab_in[i]
+        weight[0, i] = jnp.where(lab == low, 1.0, 0.0)
+        weight[1, i] = jnp.where((lab == high) & two, 1.0, 0.0)
     idg[dp, 0:1] = jnp.where(low < NOBLK, low, -1)[:, :128]
     idg[dp, 1:2] = jnp.where(two, high, -1)[:, :128]
     idg[NREP] = jnp.full((2, 128), step_ref[0], jnp.int32)
@@ -130,7 +140,7 @@
     def id_copy(j):
         dz, dc = dp_peers[j]
         return pltpu.make_async_remote_copy(
-            src_ref=idg.at[dp], dst_ref=idg.at[dp], send_sem=id_ss.at[j], recv_sem=id_rs.at[j],
+            src_ref=idg.at[dp], dst_ref=idg.at[dp], send_sem=id_ss, recv_sem=id_rs,
             device_id=(rep_peer(dz, dc), tb), device_id_type=MESH)
 
     for j in range(len(dp_peers)):
@@ -138,14 +148,20 @@
 
     def ring_copy(c, dz):
         return pltpu.make_async_remote_copy(
-            src_ref=gath.at[c, dp], dst_ref=gath.at[c, dp], send_sem=b_ss.at[c, dz - 1], recv_sem=b_rs.at[c, dz - 1],
+            src_ref=gath.at[c, dp], dst_ref=gath.at[c, dp], send_sem=b_ss, recv_sem=b_rs.at[c, dz - 1],
             device_id=(rep_peer(dz, 0), tb), device_id_type=MESH)
 
     def core_copy(c, dz):
         origin = rep_peer(dz, 0)
         return pltpu.make_async_remote_copy(
-            src_ref=gath.at[c, origin], dst_ref=gath.at[c, origin], send_sem=s_ss.at[c, dz], recv_sem=s_rs.at[c, dz],
+            src_ref=gath.at[c, origin], dst_ref=gath.at[c, origin], send_sem=s_ss, recv_sem=s_rs,
             device_id=(rep_peer(0, 1), tb), device_id_type=MESH)
+
+    def last_copy(j):
+        dz, dc = dp_peers[j]
+        return pltpu.make_async_remote_copy(
+            src_ref=gath.at[NC - 1, dp], dst_ref=gath.at[NC - 1, dp], send_sem=l_ss, recv_sem=l_rs,
+            device_id=(rep_peer(dz, dc), tb), device_id_type=MESH)
 
     def second_hop(c):
         for dz in (1, 3, 2):
@@ -155,37 +171,53 @@
     @pl.loop(0, NC)
     def _(c):
         all_blocks(c).wait_recv()
-        sum_low = jnp.zeros((RB, width), jnp.float32)
-        sum_high = jnp.zeros((RB, width), jnp.float32)
+        sum_low = jnp.zeros((RB, CW), jnp.float32)
+        sum_high = jnp.zeros((RB, CW), jnp.float32)
         for i in range(NP + 1):
-            lab = lab_in[i]
             block = inc[c, i].astype(jnp.float32)
-            sum_low += jnp.where(lab == low, 1.0, 0.0) * block
-            sum_high += jnp.where((lab == high) & two, 1.0, 0.0) * block
+            sum_low += weight[0, i] * block
+            sum_high += weight[1, i] * block
         gath[c, dp, 0] = sum_low
         gath[c, dp, 1] = sum_high
-        for dz in (1, 3, 2):
-            ring_copy(c, dz).start()
-        core_copy(c, 0).start()
-
-        @pl.when(c >= 1)
-        def _():
-            second_hop(c - 1)
-
-    second_hop(NC - 1)
-
-    for j in range(len(dp_peers)):
-        id_copy(j).wait()
+
+        @pl.when(c < NC - 1)
+        def _():
+            for dz in (1, 3, 2):
+                ring_copy(c, dz).start()
+            core_copy(c, 0).start()
+
+        @pl.when(c == NC - 1)
+        def _():
+            for j in LAST:
+                last_copy(j).start()
+
+        @pl.when(c >= LAG)
+        def _():
+            second_hop(c - LAG)
+
+    @pl.loop(NC - LAG, NC - 1)
+    def _(c):
+        second_hop(c)
+
+    others = pl.ds(0, NREP - 1)
+    pltpu.make_async_remote_copy(
+        src_ref=idg.at[others], dst_ref=idg.at[others], send_sem=id_ss, recv_sem=id_rs,
+        device_id=(rep_peer(0, 1), tb), device_id_type=MESH).wait()
     for cp in held:
         cp.wait()
 
-    @pl.loop(0, NC)
-    def _(c):
-        for dz in range(NSIDE):
-            core_copy(c, dz).wait()
-        for dz in range(1, NSIDE):
-            ring_copy(c, dz).wait_send()
-        all_blocks(c).wait_send()
+    early = pl.ds(0, NC - 1)
+    ring_sent = gath.at[early, pl.ds(0, NSIDE - 1)]
+    core_sent = gath.at[early, pl.ds(0, NSIDE)]
+    last_sent = gath.at[NC - 1, others]
+    for src, send_sem in ((ring_sent, b_ss), (stage, a_ss)):
+        pltpu.make_async_remote_copy(
+            src_ref=src, dst_ref=src, send_sem=send_sem, recv_sem=s_rs,
+            device_id=(rep_peer(0, 1), tb), device_id_type=MESH).wait_send()
+    for src, send_sem, recv_sem in ((core_sent, s_ss, s_rs), (last_sent, l_ss, l_rs)):
+        pltpu.make_async_remote_copy(
+            src_ref=src, dst_ref=src, send_sem=send_sem, recv_sem=recv_sem,
+            device_id=(rep_peer(0, 1), tb), device_id_type=MESH).wait()
 
 
 def adam_kernel(
@@ -206,8 +238,8 @@
     steps = ids_ref[NREP, 0, 0]
     power_one, power_two = lax.fori_loop(
         0, steps, lambda _, p: (p[0] * 0.9, p[1] * 0.99), (jnp.float32(1.0), jnp.float32(1.0)))
-    one = jnp.full((1, 1024), 1.0 - power_one, jnp.float32)
-    two = jnp.full((1, 1024), 1.0 - power_two, jnp.float32)
+    one = jnp.full((1, CW), 1.0 - power_one, jnp.float32)
+    two = jnp.full((1, CW), 1.0 - power_two, jnp.float32)
     rate = 0.05 / one
     scale = 1.0 / two
 
@@ -221,14 +253,15 @@
 
     def update(b, grad_of):
         for c in range(NC):
-            rows = pl.ds(pl.multiple_of(b * BROWS + c * RB, RB), RB)
+            rows = pl.ds(pl.multiple_of(b * BROWS + (c // NCOL) * RB, RB), RB)
+            cols = slice((c % NCOL) * CW, (c % NCOL + 1) * CW)
             g = grad_of(c)
-            f = 0.9 * first[rows, :] + (1.0 - 0.9) * g
-            s = 0.99 * second[rows, :] + (1.0 - 0.99) * g * g
-            new_f[rows, :] = f
-            new_s[rows, :] = s
-            moved = values[rows, :].astype(jnp.float32) - rate * f / (jnp.sqrt(scale * s) + 1e-08)
-            new_v[rows, :] = moved.astype(jnp.bfloat16)
+            f = 0.9 * first[rows, cols] + (1.0 - 0.9) * g
+            s = 0.99 * second[rows, cols] + (1.0 - 0.99) * g * g
+            new_f[rows, cols] = f
+            new_s[rows, cols] = s
+            moved = values[rows, cols].astype(jnp.float32) - rate * f / (jnp.sqrt(scale * s) + 1e-08)
+            new_v[rows, cols] = moved.astype(jnp.bfloat16)
         for cp in copies(b, new_v, new_f, new_s):
             cp.start()
 
@@ -286,7 +319,7 @@
     gath, ids, values_in, first_in, second_in = pl.pallas_call(
         exchange_kernel,
         out_shape=(
-            jax.ShapeDtypeStruct((NC, NREP, 2, RB, width), jnp.float32),
+            jax.ShapeDtypeStruct((NC, NREP, 2, RB, CW), jnp.float32),
             jax.ShapeDtypeStruct((NREP + 1, 2, 128), jnp.int32),
             like(values), like(first_moment), like(second_moment),
         ),
@@ -295,13 +328,13 @@
         scratch_shapes=[
             pltpu.SMEM(block_ids.shape, jnp.int32),
             pltpu.VMEM((SLOTS, BROWS, width), jnp.bfloat16),
-            pltpu.VMEM((NC, NP, RB, width), jnp.bfloat16),
-            pltpu.VMEM((NC, NP + 1, RB, width), jnp.bfloat16),
-            pltpu.VMEM((NP, 1, width), jnp.int32),
-            pltpu.VMEM((NP + 1, 1, width), jnp.int32),
-            dma((3,)), dma((4,)), dma((NP,)), dma((NP,)), dma((NC,)), dma((NC,)),
-            dma((NREP - 1,)), dma((NREP - 1,)), dma((NC, NSIDE - 1)), dma((NC, NSIDE - 1)),
-            dma((NC, NSIDE)), dma((NC, NSIDE)),
+            pltpu.VMEM((NC, NP, RB, CW), jnp.bfloat16),
+            pltpu.VMEM((NC, NP + 1, RB, CW), jnp.bfloat16),
+            pltpu.VMEM((NP, 1, CW), jnp.int32),
+            pltpu.VMEM((NP + 1, 1, CW), jnp.int32),
+            pltpu.VMEM((2, NP + 1, 1, CW), jnp.float32),
+            dma((1,)), dma((4,)), dma(()), dma(()), dma(()), dma((NC,)),
+            dma(()), dma(()), dma(()), dma((NC, NSIDE - 1)), dma(()), dma(()), dma(()), dma(()),
         ],
         compiler_params=pltpu.CompilerParams(
             collective_id=0, has_side_effects=True, vmem_limit_bytes=24 << 20),
@@ -313,7 +346,7 @@
         in_specs=[smem, vmem, vmem, vmem, vmem],
         out_specs=(hbm, hbm, hbm),
         scratch_shapes=[
-            pltpu.VMEM((NC, RB, width), jnp.float32),
+            pltpu.VMEM((NC, RB, CW), jnp.float32),
             pltpu.VMEM((own_rows, width), jnp.bfloat16),
             pltpu.VMEM((own_rows, width), jnp.float32),
             pltpu.VMEM((own_rows, width), jnp.float32),

time: 52.6 us -> 47.5 us (0.903)
  Pallas kernels: 50.4 us -> 45.4 us
    pallas_call x1, Pallas kernels: 45.2 us -> 40.2 us  [per_device(): pl.pallas_call(exchange_kernel, out_shape=(jax.ShapeDtypeStruct((NC, NREP...]
where the time goes in v3:
time: 47.5 us; the launch traced here: 47.3 us
  Pallas kernels  45.4 us (96%)
  between operations  1.93 us (4%)
    pallas_call x1, Pallas kernels, per_device(): pl.pallas_call(exchange_kernel, out_shape=(jax.ShapeDtypeStruct((NC, NREP...  40.2 us
    pallas_call x1, Pallas kernels, per_device(): pl.pallas_call(adam_kernel, out_shape=(like(values), like(first_moment),...  5.15 us

profile of v3, /device:TPU:1, one launch (start us, length us, event | category | flops | bytes accessed | tf_op | source)
XLA Modules:
  0.0 47.3 jit_solution(5932830535250444145)
XLA Ops:
  1.9 40.2 %exchange.1 = (f32[16,8,2,16,256]{4,3,2,1,0:T(8,128)S(1)}, s32[9,2,128]{2,1,0:T(2,128)S(1)}, bf16[1024,1024]{1,0:T(8,128)(2,1)S(1)}, f32[1024,1024]{1,0:T(8,128)S(1)}, f32[1024,1024]{1,0:T(8,128)S(1)}) custom-call(s32[1]{0:T(128)S(6)} %copy.10.cnt_ref, s32[1]{0:T(128)S(6)} %copy.11.step_ref, s32[1,8]{1,0:T(1,128)} %ids_hbm.1, ...), custom_call_target="tpu_custom_call" | custom-call | tf_op jit(solution)/shard_map/exchange/pallas_call | solution.py:319
  42.2 5.1 %adam.1 = (bf16[1024,1024]{1,0:T(8,128)(2,1)}, f32[1024,1024]{1,0:T(8,128)}, f32[1024,1024]{1,0:T(8,128)}) custom-call(s32[9,2,128]{2,1,0:T(2,128)S(1)} %get-tuple-element.8.ids_ref, f32[16,8,2,16,256]{4,3,2,1,0:T(8,128)S(1)} %get-tuple-element.9.gath, bf16[1024,1024]{1,0:T(8,128)(2,1)S(1)} %get-tuple-element.10.values, ...), custom_call_target="tpu_custom_call" | custom-call | tf_op jit(solution)/shard_map/adam/pallas_call | solution.py:343

commit v4 on v3

--- a/solution.py
+++ b/solution.py
@@ -14,11 +14,13 @@
 NROW = BROWS // RB
 NCOL = 1024 // CW
 NC = NROW * NCOL
+DIRECT = 1
+MAIN = NC - DIRECT
 PLANE = [(2, 2), (1, 2), (3, 2), (2, 1), (2, 3), (1, 1), (3, 3), (1, 3), (3, 1), (0, 2), (2, 0), (0, 1), (0, 3), (1, 0), (3, 0)]
 NP = len(PLANE)
 NREP = 8
 LAST = (4, 3, 2, 5, 1, 6, 0)
-LAG = 5
+LAG = 4
 NOBLK = 1 << 20
 
 
@@ -52,16 +54,15 @@
         pltpu.make_async_copy(first_hbm, first, ld_sem.at[2]),
         pltpu.make_async_copy(second_hbm, second, ld_sem.at[3]),
     ]
-    for cp in small:
-        cp.start()
-    load.start()
-
     barrier = pltpu.get_barrier_semaphore()
     for i in range(NP):
         pl.semaphore_signal(barrier, inc=1, device_id=(dp, owners[i]), device_id_type=MESH)
     for dz, dc in dp_peers:
         pl.semaphore_signal(barrier, inc=1, device_id=(rep_peer(dz, dc), tb), device_id_type=MESH)
 
+    for cp in small:
+        cp.start()
+    load.start()
     for cp in small:
         cp.wait()
     count = cnt_ref[0]
@@ -108,9 +109,9 @@
             block_copy(c, i).start()
         inc[c, NP] = grads[slot_of[NP], rows, cols]
 
-    send_blocks(0)
     for i in range(NP):
         label_copy(i).start()
+    send_blocks(0)
 
     @pl.loop(1, NC)
     def _(c):
@@ -157,10 +158,10 @@
             src_ref=gath.at[c, origin], dst_ref=gath.at[c, origin], send_sem=s_ss, recv_sem=s_rs,
             device_id=(rep_peer(0, 1), tb), device_id_type=MESH)
 
-    def last_copy(j):
+    def last_copy(c, j):
         dz, dc = dp_peers[j]
         return pltpu.make_async_remote_copy(
-            src_ref=gath.at[NC - 1, dp], dst_ref=gath.at[NC - 1, dp], send_sem=l_ss, recv_sem=l_rs,
+            src_ref=gath.at[c, dp], dst_ref=gath.at[c, dp], send_sem=l_ss, recv_sem=l_rs,
             device_id=(rep_peer(dz, dc), tb), device_id_type=MESH)
 
     def second_hop(c):
@@ -180,22 +181,22 @@
         gath[c, dp, 0] = sum_low
         gath[c, dp, 1] = sum_high
 
-        @pl.when(c < NC - 1)
+        @pl.when(c < MAIN)
         def _():
             for dz in (1, 3, 2):
                 ring_copy(c, dz).start()
             core_copy(c, 0).start()
 
-        @pl.when(c == NC - 1)
+        @pl.when(c >= MAIN)
         def _():
             for j in LAST:
-                last_copy(j).start()
+                last_copy(c, j).start()
 
         @pl.when(c >= LAG)
         def _():
             second_hop(c - LAG)
 
-    @pl.loop(NC - LAG, NC - 1)
+    @pl.loop(NC - LAG, MAIN)
     def _(c):
         second_hop(c)
 
@@ -206,10 +207,10 @@
     for cp in held:
         cp.wait()
 
-    early = pl.ds(0, NC - 1)
+    early = pl.ds(0, MAIN)
     ring_sent = gath.at[early, pl.ds(0, NSIDE - 1)]
     core_sent = gath.at[early, pl.ds(0, NSIDE)]
-    last_sent = gath.at[NC - 1, others]
+    last_sent = gath.at[pl.ds(MAIN, DIRECT), others]
     for src, send_sem in ((ring_sent, b_ss), (stage, a_ss)):
         pltpu.make_async_remote_copy(
             src_ref=src, dst_ref=src, send_sem=send_sem, recv_sem=s_rs,

time: 47.5 us -> 47.5 us (level)
  no operation moved by 1% of the time
where the time goes in v4:
time: 47.5 us; the launch traced here: 47.3 us
  Pallas kernels  45.4 us (96%)
  between operations  1.93 us (4%)
    pallas_call x1, Pallas kernels, per_device(): pl.pallas_call(exchange_kernel, out_shape=(jax.ShapeDtypeStruct((NC, NREP...  40.3 us
    pallas_call x1, Pallas kernels, per_device(): pl.pallas_call(adam_kernel, out_shape=(like(values), like(first_moment),...  5.15 us

profile of v4, /device:TPU:1, one launch (start us, length us, event | category | flops | bytes accessed | tf_op | source)
XLA Modules:
  0.0 47.3 jit_solution(280250703095321923)
XLA Ops:
  1.9 40.3 %exchange.1 = (f32[16,8,2,16,256]{4,3,2,1,0:T(8,128)S(1)}, s32[9,2,128]{2,1,0:T(2,128)S(1)}, bf16[1024,1024]{1,0:T(8,128)(2,1)S(1)}, f32[1024,1024]{1,0:T(8,128)S(1)}, f32[1024,1024]{1,0:T(8,128)S(1)}) custom-call(s32[1]{0:T(128)S(6)} %copy.10.cnt_ref, s32[1]{0:T(128)S(6)} %copy.11.step_ref, s32[1,8]{1,0:T(1,128)} %ids_hbm.1, ...), custom_call_target="tpu_custom_call" | custom-call | tf_op jit(solution)/shard_map/exchange/pallas_call | solution.py:320
  42.2 5.1 %adam.1 = (bf16[1024,1024]{1,0:T(8,128)(2,1)}, f32[1024,1024]{1,0:T(8,128)}, f32[1024,1024]{1,0:T(8,128)}) custom-call(s32[9,2,128]{2,1,0:T(2,128)S(1)} %get-tuple-element.8.ids_ref, f32[16,8,2,16,256]{4,3,2,1,0:T(8,128)S(1)} %get-tuple-element.9.gath, bf16[1024,1024]{1,0:T(8,128)(2,1)S(1)} %get-tuple-element.10.values, ...), custom_call_target="tpu_custom_call" | custom-call | tf_op jit(solution)/shard_map/adam/pallas_call | solution.py:344

commit v5 on v4

--- a/solution.py
+++ b/solution.py
@@ -196,9 +196,6 @@
         def _():
             second_hop(c - LAG)
 
-    @pl.loop(NC - LAG, MAIN)
-    def _(c):
-        second_hop(c)
 
     others = pl.ds(0, NREP - 1)
     pltpu.make_async_remote_copy(
@@ -206,6 +203,10 @@
         device_id=(rep_peer(0, 1), tb), device_id_type=MESH).wait()
     for cp in held:
         cp.wait()
+
+    @pl.loop(NC - LAG, MAIN)
+    def _(c):
+        second_hop(c)
 
     early = pl.ds(0, MAIN)
     ring_sent = gath.at[early, pl.ds(0, NSIDE - 1)]

time: 47.5 us -> 47.5 us (level)
  no operation moved by 1% of the time
where the time goes in v5:
time: 47.5 us; the launch traced here: 47.3 us
  Pallas kernels  45.4 us (96%)
  between operations  1.93 us (4%)
    pallas_call x1, Pallas kernels, per_device(): pl.pallas_call(exchange_kernel, out_shape=(jax.ShapeDtypeStruct((NC, NREP...  40.3 us
    pallas_call x1, Pallas kernels, per_device(): pl.pallas_call(adam_kernel, out_shape=(like(values), like(first_moment),...  5.14 us

profile of v5, /device:TPU:1, one launch (start us, length us, event | category | flops | bytes accessed | tf_op | source)
XLA Modules:
  0.0 47.3 jit_solution(11820887126907805785)
XLA Ops:
  1.9 40.3 %exchange.1 = (f32[16,8,2,16,256]{4,3,2,1,0:T(8,128)S(1)}, s32[9,2,128]{2,1,0:T(2,128)S(1)}, bf16[1024,1024]{1,0:T(8,128)(2,1)S(1)}, f32[1024,1024]{1,0:T(8,128)S(1)}, f32[1024,1024]{1,0:T(8,128)S(1)}) custom-call(s32[1]{0:T(128)S(6)} %copy.10.cnt_ref, s32[1]{0:T(128)S(6)} %copy.11.step_ref, s32[1,8]{1,0:T(1,128)} %ids_hbm.1, ...), custom_call_target="tpu_custom_call" | custom-call | tf_op jit(solution)/shard_map/exchange/pallas_call | solution.py:321
  42.2 5.1 %adam.1 = (bf16[1024,1024]{1,0:T(8,128)(2,1)}, f32[1024,1024]{1,0:T(8,128)}, f32[1024,1024]{1,0:T(8,128)}) custom-call(s32[9,2,128]{2,1,0:T(2,128)S(1)} %get-tuple-element.8.ids_ref, f32[16,8,2,16,256]{4,3,2,1,0:T(8,128)S(1)} %get-tuple-element.9.gath, bf16[1024,1024]{1,0:T(8,128)(2,1)S(1)} %get-tuple-element.10.values, ...), custom_call_target="tpu_custom_call" | custom-call | tf_op jit(solution)/shard_map/adam/pallas_call | solution.py:345
